TPU v7x, 512 devices: a whole 4x8x8 slice. The times are simulated.
512 devices in a mesh: group: 16 (over z, y_hi), rep: 32 (over x, y_lo, core).
Axes of the slice: x: 4, y: 8 (y_hi: 2, y_lo: 4; y = y_hi * 4 + y_lo), z: 8, core: 2. Of those that a mesh axis runs over, the one named last changes fastest.
Arguments:
- tokens: bfloat16 [16, 8192, 2048], P('group', 'rep'), may hold values from -6 to 6
- cotangent: bfloat16 [16, 8192, 4096], P('group', 'rep'), may hold values from -6 to 6
- gate_weight: float32 [16, 32, 256, 128], P('group', 'rep'), may hold values from -5 to 5
- up_weight: float32 [16, 32, 256, 128], P('group', 'rep'), may hold values from -5 to 5
- tile_rows: int32 [32, 2], replicated, may hold values from 0 to 15, as said below
- step: int32 [1], replicated, may hold values from 0 to 999
Outputs:
- new_gate: float32 [16, 32, 256, 128], P('group', 'rep')
Inputs may be any that keep to these rules, and one draw needn't show every extreme that they name: `tile_rows`: the 2 entries of a row are distinct, and every feature block is named by some row.
All inputs are finite; a program needn't handle non-finite values.
Results may differ from a plain program's by a relative error of at most 0.0024.
Values may be sent and summed in bfloat16 or wider, within the bound.
No kernel may reach another device: no remote copies, remote signals or barrier semaphores. Data moves between devices by JAX's collectives and lax.ppermute only.
A program may use at most 64 MiB of HBM per device.

v0:
```python
from functools import partial
import jax
import jax.numpy as jnp
from jax import lax
from jax.sharding import PartitionSpec as P

TILE = 128
PER_COL = 2
LEARNING_RATE = 0.1


def partner(value, axis, bit):
    return lax.ppermute(value, axis, [(i, i ^ 1 << bit) for i in range(lax.axis_size(axis))])


def trade(values, which_bit):
    return partner(values, "group", which_bit)


def body(tokens, cotangent, gate_weight, up_weight, tile_rows, step):
    scaling = (PER_COL * TILE) ** (-0.5)
    activations = tokens[0]
    cot_rows = cotangent[0]
    row_count = activations.shape[0]
    blocks = activations.shape[1] // TILE
    hidden = cot_rows.shape[1] // TILE
    one_hot = (tile_rows[:, :, None] == jnp.arange(blocks, dtype=jnp.int32)).astype(jnp.bfloat16)
    selected = jnp.einsum(
        "tdc,fkd->tfkc",
        activations.reshape(row_count, blocks, TILE),
        one_hot,
        preferred_element_type=jnp.float32,
    ).astype(jnp.bfloat16)
    selected = selected.reshape(row_count, hidden, PER_COL * TILE)
    master_gate = gate_weight[0]
    local_pair = jnp.concatenate([master_gate, up_weight[0]], -1).astype(jnp.bfloat16)
    combined = (
        jnp.einsum(
            "tfk,fke->tfe",
            selected,
            lax.all_gather(local_pair, "rep", axis=0, tiled=True),
            preferred_element_type=jnp.float32,
        )
        * scaling
    )
    gate_vals = combined[..., :TILE]
    up_vals = combined[..., TILE:]
    cot_blocks = cot_rows.reshape(row_count, hidden, TILE)
    sigmoid_gate = jax.nn.sigmoid(gate_vals)
    grad_gate = (
        cot_blocks * up_vals * sigmoid_gate * (1.0 + gate_vals * (1.0 - sigmoid_gate))
    ).astype(jnp.bfloat16)
    local_grad = (
        jnp.einsum("tfk,tfe->fke", selected, grad_gate, preferred_element_type=jnp.float32)
        * scaling
    )
    own_count = local_pair.shape[0]
    summed = lax.psum(local_grad, "rep")
    grad_share = lax.dynamic_slice_in_dim(summed, lax.axis_index("rep") * own_count, own_count, 0)
    stepped = master_gate - LEARNING_RATE * grad_share
    levels = lax.axis_size("group").bit_length() - 1
    chosen_bit = step[0] % levels
    branches = [partial(trade, which_bit=number) for number in range(levels)]
    partner_vals = lax.switch(chosen_bit, branches, stepped)
    averaged = 0.5 * (stepped + partner_vals)
    return averaged[None]


def solution(mesh):
    placed = (
        P("group", "rep", None),
        P("group", "rep", None),
        P("group", "rep", None, None),
        P("group", "rep", None, None),
        P(),
        P(),
    )
    return jax.shard_map(
        body, mesh=mesh, in_specs=placed, out_specs=P("group", "rep", None, None), check_vma=False
    )
```

profile of v0, /device:TPU:64, one launch (start us, length us, event | category | flops | bytes accessed | tf_op | source)
XLA Modules:
  0.0 406.5 jit_solution(12707755886064902224)
XLA Ops:
  6.5 0.0 all-gather.2.cloned.1.call-start
  6.5 1.0 bitcast_convert_fusion
  7.5 0.7 pad_maximum_fusion
  8.2 0.0 all-gather.2.cloned.1.call-update
  8.2 0.0 all-reduce.2.cloned.1.call-start
  8.3 1.5 copy.41
  9.7 3.9 convert_bitcast_fusion
  13.7 0.0 copy-start.2
  13.7 7.7 %copy.32 = bf16[256,32,2,128]{0,3,2,1:T(8,128)(2,1)} copy(bf16[256,32,2,128]{3,1,0,2:T(8,128)(2,1)} %convert_bitcast_fusion) | data formatting | bytes 8388608 | tf_op jit(solution)/shard_map/convert_element_type | solution.py:33
  21.4 0.0 copy-done.2
  21.4 3.0 copy.33
  24.4 54.1 %all-gather.2.cloned.1.call-done = bf16[32,256,256]{2,1,0:T(8,128)(2,1)} async-done(((bf16[1,256,256]{2,1,0:T(8,128)(2,1)}), bf16[32,256,256]{2,1,0:T(8,128)(2,1)}) %all-gather.2.cloned.1.call-update) | async-done | bytes 4194320 | tf_op jit(solution)/shard_map/all_gather | solution.py:41
  78.5 0.0 copy-start
  78.5 0.0 copy-start.1
  78.5 5.0 %multiply_bitcast_fusion = f32[256,32,256]{0,2,1:T(8,128)S(1)} fusion(bf16[32,256,256]{2,1,0:T(8,128)(2,1)} %all-gather.2.cloned.1.call-done, bf16[256,32,256]{0,2,1:T(8,128)(2,1)} %bitcast.31), kind=kOutput, calls=%fused_computation | convolution fusion | flops 1075838976 | bytes 16777216 | tf_op jit(solution)/shard_map/tfk,fke->tfe/dot_general | solution.py:38
  83.4 0.0 copy-done
  83.4 0.9 copy-done.1
  84.4 3.8 convolution_multiply_fusion
  88.1 0.0 copy-start.3
  88.1 0.0 all-reduce.2.cloned.1.call-update
  88.9 297.4 %all-reduce.2.cloned.1.call-done = f32[32,256,128]{2,1,0:T(8,128)} async-done(((f32[32,256,128]{2,1,0:T(8,128)}), f32[32,256,128]{2,1,0:T(8,128)}) %all-reduce.2.cloned.1.call-update) | async-done | bytes 4194320 | tf_op jit(solution)/shard_map/psum | solution.py:58
  386.3 0.0 copy-done.3
  386.3 0.9 bitcast_subtract_fusion
  387.2 10.9 %conditional.1 = (f32[1,256,128]{2,1,0:T(8,128)}) conditional(s32[]{:T(128)} %clamp.3, f32[1,256,128]{2,1,0:T(8,128)S(1)} %bitcast_subtract_fusion, f32[1,256,128]{2,1,0:T(8,128)S(1)} %bitcast_subtract_fusion, f32[1,256,128]{2,1,0:T(8,128)S(1)} %bitcast_subtract_fusion, ...), branch_computations={%region_1.2_spmd, %region_2.3_spmd, %region_3.4_spmd, %region_4.5_... | conditional | bytes 524336 | solution.py:64
  387.2 6.0 %collective-permute-start = (f32[1,256,128]{2,1,0:T(8,128)S(1)}, f32[1,256,128]{2,1,0:T(8,128)}, u32[]{:S(2)}, u32[]{:S(2)}) collective-permute-start(f32[1,256,128]{2,1,0:T(8,128)S(1)} %param), channel_id=1, source_target_pairs={{0,32},{32,0},{64,96},{96,64},{128,160},{160,128},{192,224},{224,1... | collective-permute-start | bytes 393224 | tf_op jit(solution)/shard_map/cond/branch_0_fun/ppermute | solution.py:13
  393.3 4.8 %collective-permute-done = f32[1,256,128]{2,1,0:T(8,128)} collective-permute-done((f32[1,256,128]{2,1,0:T(8,128)S(1)}, f32[1,256,128]{2,1,0:T(8,128)}, u32[]{:S(2)}, u32[]{:S(2)}) %collective-permute-start) | collective-permute-done | bytes 131104 | tf_op jit(solution)/shard_map/cond/branch_0_fun/ppermute | solution.py:13
  398.1 1.6 multiply_bitcast_fusion.1
Async XLA Ops:
  6.5 71.9 %all-gather.2.cloned.1.call-start = ((), (), s32[]{:S(2)}) async-start(), calls=%async_computation | async-start | bytes 4325376 | tf_op jit(solution)/shard_map/all_gather | solution.py:41
  8.2 378.0 %all-reduce.2.cloned.1.call-start = ((), (), s32[]{:S(2)}) async-start(), calls=%async_computation.1 | async-start | bytes 8388608 | tf_op jit(solution)/shard_map/psum | solution.py:58
  13.7 7.7 %copy-start.2 = (bf16[1,256,4096]{2,1,0:T(8,128)(2,1)S(1)}, bf16[1,256,4096]{2,1,0:T(8,128)(2,1)}, u32[]{:S(2)}) copy-start(bf16[1,256,4096]{2,1,0:T(8,128)(2,1)} %param.11) | copy-start | bytes 6291460
  78.5 5.0 %copy-start = (bf16[256,32,2,128]{0,3,2,1:T(8,128)(2,1)S(1)}, bf16[256,32,2,128]{0,3,2,1:T(8,128)(2,1)}, u32[]{:S(2)}) copy-start(bf16[256,32,2,128]{0,3,2,1:T(8,128)(2,1)} %copy.32) | copy-start | bytes 12582916
  78.5 5.9 %copy-start.1 = (f32[1,256,4096]{1,2,0:T(8,128)S(1)}, f32[1,256,4096]{1,2,0:T(8,128)}, u32[]{:S(2)}) copy-start(f32[1,256,4096]{1,2,0:T(8,128)} %copy.33) | copy-start | bytes 12582916
  88.1 298.1 %copy-start.3 = (f32[1,1,256,128]{3,2,1,0:T(8,128)S(1)}, f32[1,1,256,128]{3,2,1,0:T(8,128)}, u32[]{:S(2)}) copy-start(f32[1,1,256,128]{3,2,1,0:T(8,128)} %param.12) | copy-start | bytes 393220
  387.2 10.9 %collective-permute-start = (f32[1,256,128]{2,1,0:T(8,128)S(1)}, f32[1,256,128]{2,1,0:T(8,128)}, u32[]{:S(2)}, u32[]{:S(2)}) collective-permute-start(f32[1,256,128]{2,1,0:T(8,128)S(1)} %param), channel_id=1, source_target_pairs={{0,32},{32,0},{64,96},{96,64},{128,160},{160,128},{192,224},{224,1... | collective-permute-start | bytes 393224 | tf_op jit(solution)/shard_map/cond/branch_0_fun/ppermute | solution.py:13
Sparse Core Ops, SparseCore 0:
  9.5 68.9 all-gather.1
  88.3 297.9 all-reduce.1
where the time goes:
time: 407 us; the launch traced here: 406 us
  waiting for transfers between devices  356 us (87%)
  between operations  14.1 us (3%)
  local copies, waits for them, and re-layouts  13.1 us (3%)
  matrix products  12.6 us (3%)
  starting transfers between devices  6.09 us (1%)
  other arithmetic  4.15 us (1%)
    psum x1, waiting for transfers between devices, body(): summed = lax.psum(local_grad, 'rep')  297 us
    all_gather x1, waiting for transfers between devices, body(): lax.all_gather(local_pair, 'rep', axis=0, tiled=True)  54.1 us
  transfers between devices with their start and end apart: 3, of which 3 were waited for; matrix products, arithmetic and copies ran while one was open for 4% of the time, Pallas kernels for 0%

commit v1 on v0

--- a/solution.py
+++ b/solution.py
@@ -38,7 +38,15 @@
         jnp.einsum(
             "tfk,fke->tfe",
             selected,
-            lax.all_gather(local_pair, "rep", axis=0, tiled=True),
+            jnp.concatenate(
+                lax.all_to_all(
+                    jnp.stack([local_pair] * lax.axis_size("rep"), axis=0),
+                    axis_name="rep",
+                    split_axis=0,
+                    concat_axis=0,
+                ),
+                axis=0,
+            ),
             preferred_element_type=jnp.float32,
         )
         * scaling

time: 407 us -> 443 us (1.088)
  waiting for transfers between devices: 356 us -> 384 us
  starting transfers between devices: 6.09 us -> 14.3 us
    all_to_all x0 -> x1, waiting for transfers between devices: none -> 81.1 us  [body(): lax.all_to_all(jnp.stack([local_pair] * lax.axis_size('rep'), axis=0), ax...]
    all_gather x1 -> x0, waiting for transfers between devices: 54.1 us -> none  [body(): lax.all_gather(local_pair, 'rep', axis=0, tiled=True)]
    all_to_all x0 -> x1, starting transfers between devices: none -> 7.99 us  [body(): lax.all_to_all(jnp.stack([local_pair] * lax.axis_size('rep'), axis=0), ax...]
  transfers between devices with their start and end apart: 3 -> 3, of which waited for: 3 -> 3; matrix products, arithmetic and copies ran while one was open for 4% -> 3% of each run, Pallas kernels for 0% -> 0%
where the time goes in v1:
time: 443 us; the launch traced here: 442 us
  waiting for transfers between devices  384 us (87%)
  local copies, waits for them, and re-layouts  14.4 us (3%)
  starting transfers between devices  14.3 us (3%)
  between operations  14.2 us (3%)
  matrix products  11.8 us (3%)
    psum x1, waiting for transfers between devices, body(): summed = lax.psum(local_grad, 'rep')  298 us
    all_to_all x1, waiting for transfers between devices, body(): lax.all_to_all(jnp.stack([local_pair] * lax.axis_size('rep'), axis=0), ax...  81.1 us
  transfers between devices with their start and end apart: 3, of which 3 were waited for; matrix products, arithmetic and copies ran while one was open for 3% of the time, Pallas kernels for 0%

profile of v1, /device:TPU:64, one launch (start us, length us, event | category | flops | bytes accessed | tf_op | source)
XLA Modules:
  0.0 442.4 jit_solution(14161403738695014632)
XLA Ops:
  6.5 1.0 convert_bitcast_fusion.1
  7.5 0.1 copy.18
  7.7 2.4 stack.2
  10.1 0.0 copy-start.3
  10.1 0.0 copy-start.5
  10.1 8.0 %all-to-all-start = ((bf16[32,1,256,256]{2,3,1,0:T(8,128)(2,1)}), bf16[32,1,256,256]{2,3,1,0:T(8,128)(2,1)}, u32[]{:S(2)}, u32[]{:S(2)}) async-start(bf16[32,1,256,256]{2,3,1,0:T(8,128)(2,1)} %stack.2), calls=%async_computation | async-start | bytes 8388608 | tf_op jit(solution)/shard_map/all_to_all | solution.py:42
  18.1 0.0 all-reduce.2.cloned.1.call-start
  18.1 0.0 copy-done.3
  18.2 0.2 copy.24
  18.4 0.0 copy-done.5
  18.4 3.2 convert_bitcast_fusion
  21.6 0.0 copy-start.2
  21.6 7.7 %copy.16 = bf16[256,32,2,128]{0,3,2,1:T(8,128)(2,1)} copy(bf16[256,32,2,128]{3,1,0,2:T(8,128)(2,1)} %convert_bitcast_fusion) | data formatting | bytes 8388608 | tf_op jit(solution)/shard_map/convert_element_type | solution.py:33
  29.3 0.0 copy-done.2
  29.3 2.9 copy.17
  32.2 81.1 %all-to-all-done = bf16[32,1,256,256]{2,3,1,0:T(8,128)(2,1)} async-done(((bf16[32,1,256,256]{2,3,1,0:T(8,128)(2,1)}), bf16[32,1,256,256]{2,3,1,0:T(8,128)(2,1)}, u32[]{:S(2)}, u32[]{:S(2)}) %all-to-all-start) | async-done | bytes 4194336 | tf_op jit(solution)/shard_map/all_to_all | solution.py:42
  113.4 0.0 copy-start
  113.4 0.0 copy-start.1
  113.4 4.9 %multiply_bitcast_fusion = f32[256,32,256]{0,2,1:T(8,128)S(1)} fusion(bf16[256,32,256]{0,2,1:T(8,128)(2,1)} %bitcast.36, bf16[32,1,256,256]{2,3,1,0:T(8,128)(2,1)} %all-to-all-done), kind=kOutput, calls=%fused_computation | convolution fusion | flops 1075838976 | bytes 16777216 | tf_op jit(solution)/shard_map/tfk,fke->tfe/dot_general | solution.py:38
  118.2 0.0 copy-done
  118.2 1.0 copy-done.1
  119.3 3.8 convolution_multiply_fusion
  123.1 0.0 copy-start.4
  123.1 0.0 all-reduce.2.cloned.1.call-update
  123.8 298.2 %all-reduce.2.cloned.1.call-done = f32[32,256,128]{2,1,0:T(8,128)} async-done(((f32[32,256,128]{2,1,0:T(8,128)}), f32[32,256,128]{2,1,0:T(8,128)}) %all-reduce.2.cloned.1.call-update) | async-done | bytes 4194320 | tf_op jit(solution)/shard_map/psum | solution.py:66
  422.0 0.0 copy-done.4
  422.0 0.9 bitcast_subtract_fusion
  422.9 11.0 %conditional.1 = (f32[1,256,128]{2,1,0:T(8,128)}) conditional(s32[]{:T(128)} %clamp.3, f32[1,256,128]{2,1,0:T(8,128)S(1)} %bitcast_subtract_fusion, f32[1,256,128]{2,1,0:T(8,128)S(1)} %bitcast_subtract_fusion, f32[1,256,128]{2,1,0:T(8,128)S(1)} %bitcast_subtract_fusion, ...), branch_computations={%region_1.2_spmd, %region_2.3_spmd, %region_3.4_spmd, %region_4.5_... | conditional | bytes 524336 | solution.py:72
  422.9 6.3 %collective-permute-start = (f32[1,256,128]{2,1,0:T(8,128)S(1)}, f32[1,256,128]{2,1,0:T(8,128)}, u32[]{:S(2)}, u32[]{:S(2)}) collective-permute-start(f32[1,256,128]{2,1,0:T(8,128)S(1)} %param), channel_id=1, source_target_pairs={{0,32},{32,0},{64,96},{96,64},{128,160},{160,128},{192,224},{224,1... | collective-permute-start | bytes 393224 | tf_op jit(solution)/shard_map/cond/branch_0_fun/ppermute | solution.py:13
  429.2 4.7 %collective-permute-done = f32[1,256,128]{2,1,0:T(8,128)} collective-permute-done((f32[1,256,128]{2,1,0:T(8,128)S(1)}, f32[1,256,128]{2,1,0:T(8,128)}, u32[]{:S(2)}, u32[]{:S(2)}) %collective-permute-start) | collective-permute-done | bytes 131104 | tf_op jit(solution)/shard_map/cond/branch_0_fun/ppermute | solution.py:13
  434.0 1.6 multiply_bitcast_fusion.1
  (1 shorter events, 0.0 us)
Async XLA Ops:
  10.1 8.1 %copy-start.3 = (bf16[1,256,2048]{2,1,0:T(8,128)(2,1)S(1)}, bf16[1,256,2048]{2,1,0:T(8,128)(2,1)}, u32[]{:S(2)}) copy-start(bf16[1,256,2048]{2,1,0:T(8,128)(2,1)} %param.10) | copy-start | bytes 3145732
  10.1 8.3 %copy-start.5 = (s32[32,2]{0,1:T(2,128)S(1)}, s32[32,2]{0,1:T(2,128)}, u32[]{:S(2)}) copy-start(s32[32,2]{0,1:T(2,128)} %param.14) | copy-start | bytes 772
  10.1 103.3 %all-to-all-start = ((bf16[32,1,256,256]{2,3,1,0:T(8,128)(2,1)}), bf16[32,1,256,256]{2,3,1,0:T(8,128)(2,1)}, u32[]{:S(2)}, u32[]{:S(2)}) async-start(bf16[32,1,256,256]{2,3,1,0:T(8,128)(2,1)} %stack.2), calls=%async_computation | async-start | bytes 8388608 | tf_op jit(solution)/shard_map/all_to_all | solution.py:42
  18.1 403.9 %all-reduce.2.cloned.1.call-start = ((), (), s32[]{:S(2)}) async-start(), calls=%async_computation.1 | async-start | bytes 8388608 | tf_op jit(solution)/shard_map/psum | solution.py:66
  21.6 7.7 %copy-start.2 = (bf16[1,256,4096]{2,1,0:T(8,128)(2,1)S(1)}, bf16[1,256,4096]{2,1,0:T(8,128)(2,1)}, u32[]{:S(2)}) copy-start(bf16[1,256,4096]{2,1,0:T(8,128)(2,1)} %param.11) | copy-start | bytes 6291460
  113.4 4.9 %copy-start = (bf16[256,32,2,128]{0,3,2,1:T(8,128)(2,1)S(1)}, bf16[256,32,2,128]{0,3,2,1:T(8,128)(2,1)}, u32[]{:S(2)}) copy-start(bf16[256,32,2,128]{0,3,2,1:T(8,128)(2,1)} %copy.16) | copy-start | bytes 12582916
  113.4 5.9 %copy-start.1 = (f32[1,256,4096]{1,2,0:T(8,128)S(1)}, f32[1,256,4096]{1,2,0:T(8,128)}, u32[]{:S(2)}) copy-start(f32[1,256,4096]{1,2,0:T(8,128)} %copy.17) | copy-start | bytes 12582916
  123.1 299.0 %copy-start.4 = (f32[1,1,256,128]{3,2,1,0:T(8,128)S(1)}, f32[1,1,256,128]{3,2,1,0:T(8,128)}, u32[]{:S(2)}) copy-start(f32[1,1,256,128]{3,2,1,0:T(8,128)} %param.12) | copy-start | bytes 393220
  422.9 11.0 %collective-permute-start = (f32[1,256,128]{2,1,0:T(8,128)S(1)}, f32[1,256,128]{2,1,0:T(8,128)}, u32[]{:S(2)}, u32[]{:S(2)}) collective-permute-start(f32[1,256,128]{2,1,0:T(8,128)S(1)} %param), channel_id=1, source_target_pairs={{0,32},{32,0},{64,96},{96,64},{128,160},{160,128},{192,224},{224,1... | collective-permute-start | bytes 393224 | tf_op jit(solution)/shard_map/cond/branch_0_fun/ppermute | solution.py:13
Sparse Core Ops, SparseCore 0:
  123.2 298.7 all-reduce.1
